TPU v7x, 128 devices: a whole 4x4x4 slice. The times are simulated.
128 devices in a mesh: tm: 8 (over z_hi, x), space: 16 (over z_lo, y, core).
Axes of the slice: x: 4, y: 4, z: 4 (z_hi: 2, z_lo: 2; z = z_hi * 2 + z_lo), core: 2. Of those that a mesh axis runs over, the one named last changes fastest.
Arguments:
- snapshots: float32 [256, 3, 16, 32, 128], P('tm', None, 'space'), may hold values from -6 to 6
- coeffs: float32 [256, 128], replicated, may hold values from -0.375 to 0.375
- pair_table: int32 [4096, 2], replicated, may hold values from 0 to 127
Outputs:
- tensor: float32 [4096, 128], P(('tm', 'space'))
Inputs may be any that keep to these rules, and one draw needn't show every extreme that they name: `pair_table`: column 0 names the carrying mode, column 1 the carried mode.
All inputs are finite; a program needn't handle non-finite values.
Results may differ from a plain program's by a relative error of at most 0.00016.
Values sent between devices are 32-bit elements; how exact they have to be, the bound alone decides.
A program may use at most 192 MiB of HBM per device.

v0:
```python
import math
import jax
import jax.numpy as jnp
from jax import lax
from jax.sharding import PartitionSpec as P


def padded(block, sides, width):
    for axis, dim in sides:
        count = lax.axis_size(axis)
        forward = [(i, i + 1) for i in range(count - 1)]
        forward.append((count - 1, 0))
        backward = [(target, source) for source, target in forward]
        low = lax.ppermute(
            lax.slice_in_dim(block, block.shape[dim] - width, None, axis=dim), axis, forward
        )
        high = lax.ppermute(lax.slice_in_dim(block, 0, width, axis=dim), axis, backward)
        block = jnp.concatenate([low, block, high], axis=dim)
    return block


def slope_field(center, padded_x, padded_y):
    stream_slope = (padded_x[:, :, 2:] - padded_x[:, :, :-2]) * 0.5
    normal_slope = (padded_y[:, :, :, 2:] - padded_y[:, :, :, :-2]) * 0.5
    span_slope = (jnp.roll(center, -1, 4) - jnp.roll(center, 1, 4)) * 0.5
    return jnp.stack([stream_slope, normal_slope, span_slope], axis=1)


def pair_block(pair_rows, table_modes, table_slopes, flat_modes):
    modes_count = table_modes.shape[0]
    cells = flat_modes.shape[2]
    group_size = pair_rows.shape[0]
    levels = lax.broadcasted_iota(jnp.int32, (group_size, modes_count), 1)
    first_pick = (pair_rows[:, 0:1] == levels).astype(jnp.float32)
    second_pick = (pair_rows[:, 1:2] == levels).astype(jnp.float32)
    first_modes = jnp.dot(
        first_pick, table_modes, precision=lax.Precision.HIGHEST, preferred_element_type=jnp.float32
    ).reshape(group_size, 3, cells)
    second_slopes = jnp.dot(
        second_pick,
        table_slopes,
        precision=lax.Precision.HIGHEST,
        preferred_element_type=jnp.float32,
    ).reshape(group_size, 3, 3, cells)
    convection = jnp.einsum(
        "bdl,bdcl->bcl", first_modes, second_slopes, precision=lax.Precision.HIGHEST
    )
    return jnp.einsum("bcl,kcl->bk", convection, flat_modes, precision=lax.Precision.HIGHEST)


def pair_terms(pair_source, flat_modes, flat_slopes, factor, row_count):
    modes_count = flat_modes.shape[0]
    table_modes = flat_modes.reshape(modes_count, -1)
    table_slopes = flat_slopes.reshape(modes_count, -1)
    group_size = math.gcd(row_count, 64)
    grouped = pair_source.reshape(row_count // group_size, group_size, 2)

    def one_group(group_rows):
        return pair_block(group_rows, table_modes, table_slopes, flat_modes)

    result = lax.map(one_group, grouped)
    return result.reshape(row_count, -1) * factor


def shards(snapshots, coeffs, pair_table):
    mode_field = jnp.einsum(
        "sk,scxyz->kcxyz",
        coeffs,
        lax.all_to_all(snapshots, "tm", split_axis=3, concat_axis=0, tiled=True),
        precision=lax.Precision.HIGHEST,
    )
    tm_count = lax.axis_size("tm")
    space_count = lax.axis_size("space")
    total_cells = (
        mode_field.shape[2] * mode_field.shape[3] * mode_field.shape[4] * tm_count * space_count
    )
    factor = float(total_cells) ** (-0.5)
    modes_count = mode_field.shape[0]
    whole_slab = lax.all_gather(mode_field, "tm", axis=3, tiled=True)
    padded_x = padded(whole_slab, (("space", 2),), 1)
    padded_y = jnp.pad(whole_slab, ((0, 0), (0, 0), (0, 0), (1, 1), (0, 0)))
    slopes = slope_field(whole_slab, padded_x, padded_y)
    flat_modes = whole_slab.reshape(modes_count, 3, -1)
    flat_slopes = slopes.reshape(modes_count, 3, 3, -1)
    owned_count = pair_table.shape[0] // tm_count
    owned = lax.dynamic_slice_in_dim(pair_table, lax.axis_index("tm") * owned_count, owned_count, 0)
    tensor = lax.psum_scatter(
        pair_terms(
            owned,
            flat_modes,
            flat_slopes,
            factor,
            lax.axis_size("space") * (owned_count // space_count),
        ),
        "space",
        scatter_dimension=0,
        tiled=True,
    )
    return tensor


def solution(mesh):
    placed = (P("tm", None, "space", None, None), P(), P())
    return jax.shard_map(
        shards, mesh=mesh, in_specs=placed, out_specs=P(("tm", "space"), None), check_vma=False
    )
```

profile of v0, /device:TPU:0, one launch (start us, length us, event | category | flops | bytes accessed | tf_op | source)
XLA Modules:
  0.0 765.1 jit_solution(8880501986956262538)
XLA Ops:
  8.9 30.3 %all_to_all.15 = f32[32,3,1,32,128]{4,0,2,1,3:T(8,128)S(1)} all-to-all(f32[32,3,1,32,128]{4,0,2,1,3:T(8,128)S(1)} %copy.44), channel_id=1, replica_groups=mesh['tm'=8,'space'=16] {'tm'}, dimensions={3} | all-to-all | bytes 3145728 | tf_op jit(solution)/shard_map/all_to_all | solution.py:69
  41.5 86.9 %all-gather.3.cloned.1.call-done = f32[128,3,32,128]{3,0,2,1:T(8,128)} async-done(((f32[128,3,4,128]{3,0,2,1:T(8,128)}), f32[128,3,32,128]{3,0,2,1:T(8,128)}) %all-gather.3.cloned.1.call-update) | async-done | bytes 6291472 | tf_op jit(solution)/shard_map/all_gather | solution.py:79
  130.8 6.7 copy.51
  137.5 6.6 copy.55
  144.1 6.8 copy.56
  150.8 9.3 %fusion.15 = f32[128,1,3,1,32,128]{5,0,4,2,3,1:T(8,128)} fusion(f32[128,3,1,32,128]{4,0,3,1,2:T(8,128)} %bitcast.73), kind=kLoop, calls=%fused_computation.20 | loop fusion | flops 3145728 | bytes 12582912 | tf_op jit(solution)/shard_map/stack | solution.py:26
  160.2 6.6 slice_bitcast_fusion.3
  166.8 6.7 slice_bitcast_fusion.2
  173.5 10.1 %fusion.16 = f32[128,1,3,1,32,128]{5,0,4,2,3,1:T(8,128)S(1)} fusion(f32[128,1,3,1,32,1]{5,0,4,2,3,1:T(8,128)} %get-tuple-element.77, f32[128,1,3,1,32,127]{5,0,4,2,3,1:T(8,128)} %get-tuple-element.79, f32[128,1,3,1,32,127]{5,0,4,2,3,1:T(8,128)} %get-tuple-element.78, f32[128,1,3,1,32,1]{5,0,4,2,3,1:T(8,128)} %get-tuple-element.76), kind=kLoop, calls=%fused_computation.26 | loop fusion | flops 6291456 | bytes 18874368 | tf_op jit(solution)/shard_map/mul | solution.py:25
  183.6 15.2 %collective-permute-done = f32[128,3,1,32,128]{4,0,3,1,2:T(8,128)} collective-permute-done((f32[128,3,1,32,128]{4,0,3,1,2:T(8,128)}, f32[128,3,1,32,128]{4,0,3,1,2:T(8,128)}, u32[]{:S(2)}, u32[]{:S(2)}) %collective-permute-start) | collective-permute-done | bytes 6291488 | tf_op jit(solution)/shard_map/ppermute | solution.py:17
  202.8 6.0 multiply_bitcast_fusion
  208.8 6.7 pad_maximum_fusion
  215.5 18.7 %copy.50 = f32[128,3,3,1,32,128]{0,5,4,2,1,3:T(8,128)} copy(f32[128,3,3,1,32,128]{5,0,4,2,3,1:T(8,128)} %pad_maximum_fusion) | data formatting | bytes 37748736 | tf_op jit(solution)/shard_map/stack | solution.py:26
  234.2 18.7 %copy.54 = f32[128,36864]{1,0:T(8,128)} copy(f32[128,36864]{0,1:T(8,128)} %bitcast.78) | data formatting | bytes 37748736 | tf_op jit(solution)/shard_map/while | solution.py:61
  252.9 447.4 %while.10 = (s32[]{:T(128)}, f32[8,64,128]{2,1,0:T(8,128)S(1)}, s32[8,64,2]{1,0,2:T(8,128)S(1)}, f32[128,36864]{1,0:T(8,128)}, f32[128,12288]{1,0:T(8,128)}, /*index=5*/f32[128,3,4096]{2,0,1:T(8,128)}, s32[]{:T(128)}) while((s32[]{:T(128)}, f32[8,64,128]{2,1,0:T(8,128)S(1)}, s32[8,64,2]{1,0,2:T(8,128)S(1)}, f32[128,36864]{1,0:T(8,128)}, ...), condition=%wide.region_1.2_spmd, body=%wide.region_0.1_spmd.sunk | while | flops 6043746304 | bytes 89164368 | solution.py:61
  252.9 13.5 %fusion.34 = f32[64,36864]{1,0:T(8,128)} fusion(f32[128,36864]{1,0:T(8,128)} %get-tuple-element.138, s32[64]{0:T(128)S(1)} %get-tuple-element.119), kind=kOutput, calls=%fused_computation.8.clone.1 | convolution fusion | flops 3623886848 | bytes 28311808 | tf_op jit(solution)/shard_map/while/body/eval_jaxpr/dot_general | solution.py:39
  266.5 12.7 %reshape.108 = f32[64,3,3,4096]{3,2,1,0:T(4,128)} reshape(f32[64,36864]{1,0:T(8,128)} %fusion.34) | data formatting | bytes 18874368 | tf_op jit(solution)/shard_map/while/body/eval_jaxpr/reshape | solution.py:44
  287.4 12.6 %multiply_reduce_fusion.2 = f32[64,4096,3]{1,2,0:T(4,128)S(1)} fusion(f32[64,3,3,4096]{3,2,1,0:T(4,128)} %reshape.108, f32[64,4096,3]{1,2,0:T(4,128)} %bitcast.70), kind=kLoop, calls=%fused_computation.clone.1 | loop fusion | flops 3932160 | bytes 15728640 | tf_op jit(solution)/shard_map/while
  299.9 8.9 %fusion.36 = f32[8,64,128]{2,1,0:T(8,128)S(1)} fusion(f32[8,64,128]{2,1,0:T(8,128)S(1)} %get-tuple-element.129, s32[]{:T(128)} %get-tuple-element.128, f32[128,3,4096]{2,0,1:T(8,128)} %get-tuple-element.140, f32[64,4096,3]{1,2,0:T(4,128)S(1)} %multiply_reduce_fusion.2), kind=kOutput, calls=%fused_computation.5.clone.1 | convolution fusion | flops 1207959552 | bytes 10518532 | tf_op jit(solution)/shard_map/while/body/eval_jaxpr/bcl,kcl->bk/dot_general | solution.py:48
  308.9 13.5 %fusion.34 = f32[64,36864]{1,0:T(8,128)} fusion(f32[128,36864]{1,0:T(8,128)} %get-tuple-element.138, s32[64]{0:T(128)S(1)} %get-tuple-element.119), kind=kOutput, calls=%fused_computation.8.clone.1 | convolution fusion | flops 3623886848 | bytes 28311808 | tf_op jit(solution)/shard_map/while/body/eval_jaxpr/dot_general | solution.py:39
  322.4 12.7 %reshape.108 = f32[64,3,3,4096]{3,2,1,0:T(4,128)} reshape(f32[64,36864]{1,0:T(8,128)} %fusion.34) | data formatting | bytes 18874368 | tf_op jit(solution)/shard_map/while/body/eval_jaxpr/reshape | solution.py:44
  343.3 12.6 %multiply_reduce_fusion.2 = f32[64,4096,3]{1,2,0:T(4,128)S(1)} fusion(f32[64,3,3,4096]{3,2,1,0:T(4,128)} %reshape.108, f32[64,4096,3]{1,2,0:T(4,128)} %bitcast.70), kind=kLoop, calls=%fused_computation.clone.1 | loop fusion | flops 3932160 | bytes 15728640 | tf_op jit(solution)/shard_map/while
  355.9 8.9 %fusion.36 = f32[8,64,128]{2,1,0:T(8,128)S(1)} fusion(f32[8,64,128]{2,1,0:T(8,128)S(1)} %get-tuple-element.129, s32[]{:T(128)} %get-tuple-element.128, f32[128,3,4096]{2,0,1:T(8,128)} %get-tuple-element.140, f32[64,4096,3]{1,2,0:T(4,128)S(1)} %multiply_reduce_fusion.2), kind=kOutput, calls=%fused_computation.5.clone.1 | convolution fusion | flops 1207959552 | bytes 10518532 | tf_op jit(solution)/shard_map/while/body/eval_jaxpr/bcl,kcl->bk/dot_general | solution.py:48
  364.8 13.5 %fusion.34 = f32[64,36864]{1,0:T(8,128)} fusion(f32[128,36864]{1,0:T(8,128)} %get-tuple-element.138, s32[64]{0:T(128)S(1)} %get-tuple-element.119), kind=kOutput, calls=%fused_computation.8.clone.1 | convolution fusion | flops 3623886848 | bytes 28311808 | tf_op jit(solution)/shard_map/while/body/eval_jaxpr/dot_general | solution.py:39
  378.3 12.7 %reshape.108 = f32[64,3,3,4096]{3,2,1,0:T(4,128)} reshape(f32[64,36864]{1,0:T(8,128)} %fusion.34) | data formatting | bytes 18874368 | tf_op jit(solution)/shard_map/while/body/eval_jaxpr/reshape | solution.py:44
  399.2 12.6 %multiply_reduce_fusion.2 = f32[64,4096,3]{1,2,0:T(4,128)S(1)} fusion(f32[64,3,3,4096]{3,2,1,0:T(4,128)} %reshape.108, f32[64,4096,3]{1,2,0:T(4,128)} %bitcast.70), kind=kLoop, calls=%fused_computation.clone.1 | loop fusion | flops 3932160 | bytes 15728640 | tf_op jit(solution)/shard_map/while
  411.8 8.9 %fusion.36 = f32[8,64,128]{2,1,0:T(8,128)S(1)} fusion(f32[8,64,128]{2,1,0:T(8,128)S(1)} %get-tuple-element.129, s32[]{:T(128)} %get-tuple-element.128, f32[128,3,4096]{2,0,1:T(8,128)} %get-tuple-element.140, f32[64,4096,3]{1,2,0:T(4,128)S(1)} %multiply_reduce_fusion.2), kind=kOutput, calls=%fused_computation.5.clone.1 | convolution fusion | flops 1207959552 | bytes 10518532 | tf_op jit(solution)/shard_map/while/body/eval_jaxpr/bcl,kcl->bk/dot_general | solution.py:48
  420.7 13.5 %fusion.34 = f32[64,36864]{1,0:T(8,128)} fusion(f32[128,36864]{1,0:T(8,128)} %get-tuple-element.138, s32[64]{0:T(128)S(1)} %get-tuple-element.119), kind=kOutput, calls=%fused_computation.8.clone.1 | convolution fusion | flops 3623886848 | bytes 28311808 | tf_op jit(solution)/shard_map/while/body/eval_jaxpr/dot_general | solution.py:39
  434.2 12.7 %reshape.108 = f32[64,3,3,4096]{3,2,1,0:T(4,128)} reshape(f32[64,36864]{1,0:T(8,128)} %fusion.34) | data formatting | bytes 18874368 | tf_op jit(solution)/shard_map/while/body/eval_jaxpr/reshape | solution.py:44
  455.1 12.6 %multiply_reduce_fusion.2 = f32[64,4096,3]{1,2,0:T(4,128)S(1)} fusion(f32[64,3,3,4096]{3,2,1,0:T(4,128)} %reshape.108, f32[64,4096,3]{1,2,0:T(4,128)} %bitcast.70), kind=kLoop, calls=%fused_computation.clone.1 | loop fusion | flops 3932160 | bytes 15728640 | tf_op jit(solution)/shard_map/while
  467.7 8.9 %fusion.36 = f32[8,64,128]{2,1,0:T(8,128)S(1)} fusion(f32[8,64,128]{2,1,0:T(8,128)S(1)} %get-tuple-element.129, s32[]{:T(128)} %get-tuple-element.128, f32[128,3,4096]{2,0,1:T(8,128)} %get-tuple-element.140, f32[64,4096,3]{1,2,0:T(4,128)S(1)} %multiply_reduce_fusion.2), kind=kOutput, calls=%fused_computation.5.clone.1 | convolution fusion | flops 1207959552 | bytes 10518532 | tf_op jit(solution)/shard_map/while/body/eval_jaxpr/bcl,kcl->bk/dot_general | solution.py:48
  476.6 13.5 %fusion.34 = f32[64,36864]{1,0:T(8,128)} fusion(f32[128,36864]{1,0:T(8,128)} %get-tuple-element.138, s32[64]{0:T(128)S(1)} %get-tuple-element.119), kind=kOutput, calls=%fused_computation.8.clone.1 | convolution fusion | flops 3623886848 | bytes 28311808 | tf_op jit(solution)/shard_map/while/body/eval_jaxpr/dot_general | solution.py:39
  490.2 12.7 %reshape.108 = f32[64,3,3,4096]{3,2,1,0:T(4,128)} reshape(f32[64,36864]{1,0:T(8,128)} %fusion.34) | data formatting | bytes 18874368 | tf_op jit(solution)/shard_map/while/body/eval_jaxpr/reshape | solution.py:44
  511.1 12.6 %multiply_reduce_fusion.2 = f32[64,4096,3]{1,2,0:T(4,128)S(1)} fusion(f32[64,3,3,4096]{3,2,1,0:T(4,128)} %reshape.108, f32[64,4096,3]{1,2,0:T(4,128)} %bitcast.70), kind=kLoop, calls=%fused_computation.clone.1 | loop fusion | flops 3932160 | bytes 15728640 | tf_op jit(solution)/shard_map/while
  523.6 8.9 %fusion.36 = f32[8,64,128]{2,1,0:T(8,128)S(1)} fusion(f32[8,64,128]{2,1,0:T(8,128)S(1)} %get-tuple-element.129, s32[]{:T(128)} %get-tuple-element.128, f32[128,3,4096]{2,0,1:T(8,128)} %get-tuple-element.140, f32[64,4096,3]{1,2,0:T(4,128)S(1)} %multiply_reduce_fusion.2), kind=kOutput, calls=%fused_computation.5.clone.1 | convolution fusion | flops 1207959552 | bytes 10518532 | tf_op jit(solution)/shard_map/while/body/eval_jaxpr/bcl,kcl->bk/dot_general | solution.py:48
  532.6 13.5 %fusion.34 = f32[64,36864]{1,0:T(8,128)} fusion(f32[128,36864]{1,0:T(8,128)} %get-tuple-element.138, s32[64]{0:T(128)S(1)} %get-tuple-element.119), kind=kOutput, calls=%fused_computation.8.clone.1 | convolution fusion | flops 3623886848 | bytes 28311808 | tf_op jit(solution)/shard_map/while/body/eval_jaxpr/dot_general | solution.py:39
  546.1 12.7 %reshape.108 = f32[64,3,3,4096]{3,2,1,0:T(4,128)} reshape(f32[64,36864]{1,0:T(8,128)} %fusion.34) | data formatting | bytes 18874368 | tf_op jit(solution)/shard_map/while/body/eval_jaxpr/reshape | solution.py:44
  567.0 12.6 %multiply_reduce_fusion.2 = f32[64,4096,3]{1,2,0:T(4,128)S(1)} fusion(f32[64,3,3,4096]{3,2,1,0:T(4,128)} %reshape.108, f32[64,4096,3]{1,2,0:T(4,128)} %bitcast.70), kind=kLoop, calls=%fused_computation.clone.1 | loop fusion | flops 3932160 | bytes 15728640 | tf_op jit(solution)/shard_map/while
  579.6 8.9 %fusion.36 = f32[8,64,128]{2,1,0:T(8,128)S(1)} fusion(f32[8,64,128]{2,1,0:T(8,128)S(1)} %get-tuple-element.129, s32[]{:T(128)} %get-tuple-element.128, f32[128,3,4096]{2,0,1:T(8,128)} %get-tuple-element.140, f32[64,4096,3]{1,2,0:T(4,128)S(1)} %multiply_reduce_fusion.2), kind=kOutput, calls=%fused_computation.5.clone.1 | convolution fusion | flops 1207959552 | bytes 10518532 | tf_op jit(solution)/shard_map/while/body/eval_jaxpr/bcl,kcl->bk/dot_general | solution.py:48
  588.5 13.5 %fusion.34 = f32[64,36864]{1,0:T(8,128)} fusion(f32[128,36864]{1,0:T(8,128)} %get-tuple-element.138, s32[64]{0:T(128)S(1)} %get-tuple-element.119), kind=kOutput, calls=%fused_computation.8.clone.1 | convolution fusion | flops 3623886848 | bytes 28311808 | tf_op jit(solution)/shard_map/while/body/eval_jaxpr/dot_general | solution.py:39
  602.0 12.7 %reshape.108 = f32[64,3,3,4096]{3,2,1,0:T(4,128)} reshape(f32[64,36864]{1,0:T(8,128)} %fusion.34) | data formatting | bytes 18874368 | tf_op jit(solution)/shard_map/while/body/eval_jaxpr/reshape | solution.py:44
  622.9 12.6 %multiply_reduce_fusion.2 = f32[64,4096,3]{1,2,0:T(4,128)S(1)} fusion(f32[64,3,3,4096]{3,2,1,0:T(4,128)} %reshape.108, f32[64,4096,3]{1,2,0:T(4,128)} %bitcast.70), kind=kLoop, calls=%fused_computation.clone.1 | loop fusion | flops 3932160 | bytes 15728640 | tf_op jit(solution)/shard_map/while
  635.5 8.9 %fusion.36 = f32[8,64,128]{2,1,0:T(8,128)S(1)} fusion(f32[8,64,128]{2,1,0:T(8,128)S(1)} %get-tuple-element.129, s32[]{:T(128)} %get-tuple-element.128, f32[128,3,4096]{2,0,1:T(8,128)} %get-tuple-element.140, f32[64,4096,3]{1,2,0:T(4,128)S(1)} %multiply_reduce_fusion.2), kind=kOutput, calls=%fused_computation.5.clone.1 | convolution fusion | flops 1207959552 | bytes 10518532 | tf_op jit(solution)/shard_map/while/body/eval_jaxpr/bcl,kcl->bk/dot_general | solution.py:48
  644.4 13.5 %fusion.34 = f32[64,36864]{1,0:T(8,128)} fusion(f32[128,36864]{1,0:T(8,128)} %get-tuple-element.138, s32[64]{0:T(128)S(1)} %get-tuple-element.119), kind=kOutput, calls=%fused_computation.8.clone.1 | convolution fusion | flops 3623886848 | bytes 28311808 | tf_op jit(solution)/shard_map/while/body/eval_jaxpr/dot_general | solution.py:39
  657.9 12.7 %reshape.108 = f32[64,3,3,4096]{3,2,1,0:T(4,128)} reshape(f32[64,36864]{1,0:T(8,128)} %fusion.34) | data formatting | bytes 18874368 | tf_op jit(solution)/shard_map/while/body/eval_jaxpr/reshape | solution.py:44
  678.8 12.6 %multiply_reduce_fusion.2 = f32[64,4096,3]{1,2,0:T(4,128)S(1)} fusion(f32[64,3,3,4096]{3,2,1,0:T(4,128)} %reshape.108, f32[64,4096,3]{1,2,0:T(4,128)} %bitcast.70), kind=kLoop, calls=%fused_computation.clone.1 | loop fusion | flops 3932160 | bytes 15728640 | tf_op jit(solution)/shard_map/while
  691.4 8.9 %fusion.36 = f32[8,64,128]{2,1,0:T(8,128)S(1)} fusion(f32[8,64,128]{2,1,0:T(8,128)S(1)} %get-tuple-element.129, s32[]{:T(128)} %get-tuple-element.128, f32[128,3,4096]{2,0,1:T(8,128)} %get-tuple-element.140, f32[64,4096,3]{1,2,0:T(4,128)S(1)} %multiply_reduce_fusion.2), kind=kOutput, calls=%fused_computation.5.clone.1 | convolution fusion | flops 1207959552 | bytes 10518532 | tf_op jit(solution)/shard_map/while/body/eval_jaxpr/bcl,kcl->bk/dot_general | solution.py:48
  701.0 57.3 %reduce-scatter.2.cloned.1.call-done = f32[32,128]{1,0:T(8,128)} async-done(((f32[512,128]{1,0:T(8,128)}), f32[32,128]{1,0:T(8,128)}) %reduce-scatter.2.cloned.1.call-update) | async-done | bytes 16400 | tf_op jit(solution)/shard_map/reduce_scatter | solution.py:87
  (61 shorter events, 77.7 us)
Async XLA Ops:
  6.5 33.0 %copy-start = (f32[256,128]{1,0:T(8,128)S(1)}, f32[256,128]{1,0:T(8,128)}, u32[]{:S(2)}) copy-start(f32[256,128]{1,0:T(8,128)} %param.6) | copy-start | bytes 393220
  6.5 121.9 %all-gather.3.cloned.1.call-start = ((), (), s32[]{:S(2)}) async-start(), calls=%async_computation.3 | async-start | bytes 7077888 | tf_op jit(solution)/shard_map/all_gather | solution.py:79
  41.5 716.8 %reduce-scatter.2.cloned.1.call-start = ((), (), s32[]{:S(2)}) async-start(), calls=%async_computation.2 | async-start | bytes 278528 | tf_op jit(solution)/shard_map/reduce_scatter | solution.py:87
  128.4 70.4 %collective-permute-start = (f32[128,3,1,32,128]{4,0,3,1,2:T(8,128)}, f32[128,3,1,32,128]{4,0,3,1,2:T(8,128)}, u32[]{:S(2)}, u32[]{:S(2)}) collective-permute-start(f32[128,3,1,32,128]{4,0,3,1,2:T(8,128)} %bitcast.71), channel_id=1, source_target_pairs={{1,0},{2,1},{3,2},{4,3},{5,4},{6,5},{7,6},{8,7},{9,8},{10,9},{11,1... | collective-permute-start | bytes 18874376 | tf_op jit(solution)/shard_map/ppermute | solution.py:17
  130.0 72.8 %collective-permute-start.1 = (f32[128,3,1,32,128]{4,0,3,1,2:T(8,128)}, f32[128,3,1,32,128]{4,0,3,1,2:T(8,128)}, u32[]{:S(2)}, u32[]{:S(2)}) collective-permute-start(f32[128,3,1,32,128]{4,0,3,1,2:T(8,128)} %bitcast.72), channel_id=1, source_target_pairs={{0,1},{1,2},{2,3},{3,4},{4,5},{5,6},{6,7},{7,8},{8,9},{9,10},{10,1... | collective-permute-start | bytes 18874376 | tf_op jit(solution)/shard_map/ppermute | solution.py:14
  144.1 16.1 %slice-start = ((s8[6291456]{0:T(1024)(128)(4,1)}), s8[2097152]{0:T(1024)(128)(4,1)S(1)}, s32[]{:S(2)}) async-start(s8[6291456]{0:T(1024)(128)(4,1)} %bitcast.74), calls=%async_computation.4 | async-start | bytes 4194304
  150.8 9.3 %slice-start.1 = ((s8[6291456]{0:T(1024)(128)(4,1)}), s8[4194304]{0:T(1024)(128)(4,1)S(1)}, s32[]{:S(2)}) async-start(s8[6291456]{0:T(1024)(128)(4,1)} %bitcast.74), calls=%async_computation.5 | async-start | bytes 8388608
  173.5 35.3 %slice-start.2 = ((s8[6291456]{0:T(1024)(128)(4,1)}), s8[4194304]{0:T(1024)(128)(4,1)S(1)}, s32[]{:S(2)}) async-start(s8[6291456]{0:T(1024)(128)(4,1)} %bitcast.81), calls=%async_computation.6 | async-start | bytes 8388608
  173.5 35.3 %slice-start.3 = ((s8[6291456]{0:T(1024)(128)(4,1)}), s8[2097152]{0:T(1024)(128)(4,1)S(1)}, s32[]{:S(2)}) async-start(s8[6291456]{0:T(1024)(128)(4,1)} %bitcast.81), calls=%async_computation.7 | async-start | bytes 4194304
  700.3 58.0 %copy-start.1 = (f32[256,128]{1,0:T(8,128)S(1)}, f32[256,128]{1,0:T(8,128)}, u32[]{:S(2)}) copy-start(f32[256,128]{1,0:T(8,128)} %param.6) | copy-start | bytes 393220
Sparse Core Ops, SparseCore 0:
  41.6 86.7 all-gather.2
  701.2 57.0 reduce-scatter.1
where the time goes:
time: 769 us; the launch traced here: 765 us
  matrix products  217 us (28%)
  local copies, waits for them, and re-layouts  205 us (27%)
  waiting for transfers between devices  163 us (21%)
  other arithmetic  133 us (17%)
  blocking collectives  30.3 us (4%)
  between operations  13.5 us (2%)
    dot_general x8, matrix products, pair_block(): jnp.dot(second_pick, table_slopes, precision=lax.Precision.HIGHEST, prefe...  108 us
    reshape x8, local copies, waits for them, and re-layouts, pair_block(): second_slopes = jnp.dot(second_pick, table_slopes, precision=lax.Precisio...  101 us
    while x8, other arithmetic  101 us
    all_gather x1, waiting for transfers between devices, shards(): whole_slab = lax.all_gather(mode_field, 'tm', axis=3, tiled=True)  86.9 us
    dot_general x8, matrix products, pair_block(): jnp.einsum('bcl,kcl->bk', convection, flat_modes, precision=lax.Precision...  70.9 us
    reduce_scatter x1, waiting for transfers between devices, shards(): lax.psum_scatter(pair_terms(owned, flat_modes, flat_slopes, factor, lax.a...  57.3 us
    dot_general x8, matrix products, pair_block(): jnp.dot(first_pick, table_modes, precision=lax.Precision.HIGHEST, preferr...  36.1 us
    while x3, local copies, waits for them, and re-layouts, pair_terms(): result = lax.map(one_group, grouped)  32.1 us
  transfers between devices with their start and end apart: 4, of which 4 were waited for; matrix products, arithmetic and copies ran while one was open for 7% of the time, Pallas kernels for 0%

commit v1 on v0

--- a/solution.py
+++ b/solution.py
@@ -76,7 +76,8 @@
     )
     factor = float(total_cells) ** (-0.5)
     modes_count = mode_field.shape[0]
-    whole_slab = lax.all_gather(mode_field, "tm", axis=3, tiled=True)
+    repeated = jnp.stack([mode_field] * lax.axis_size("tm"))
+    whole_slab = jnp.concatenate(lax.all_to_all(repeated, "tm", 0, 0), axis=3)
     padded_x = padded(whole_slab, (("space", 2),), 1)
     padded_y = jnp.pad(whole_slab, ((0, 0), (0, 0), (0, 0), (1, 1), (0, 0)))
     slopes = slope_field(whole_slab, padded_x, padded_y)

time: 769 us -> 762 us (level)
  blocking collectives: 30.3 us -> 105 us
  waiting for transfers between devices: 163 us -> 99.5 us
  other arithmetic: 133 us -> 117 us
    all_gather x1 -> x0, waiting for transfers between devices: 86.9 us -> none  [shards(): whole_slab = lax.all_gather(mode_field, 'tm', axis=3, tiled=True)]
    all_to_all x0 -> x1, blocking collectives: none -> 75.1 us  [shards(): whole_slab = jnp.concatenate(lax.all_to_all(repeated, 'tm', 0, 0), axis=3)]
    ppermute x1, waiting for transfers between devices: 15.2 us -> 39.5 us  [padded(): lax.ppermute(lax.slice_in_dim(block, 0, width, axis=dim), axis, backward)]
    mul x1, other arithmetic: 10.1 us -> 1.64 us  [slope_field(): span_slope = (jnp.roll(center, -1, 4) - jnp.roll(center, 1, 4)) * 0.5]
    another operation x3, other arithmetic: 22 us -> 14.2 us  [slope_field(): return jnp.stack([stream_slope, normal_slope, span_slope], axis=1)]
  transfers between devices with their start and end apart: 4 -> 3, of which waited for: 4 -> 3; matrix products, arithmetic and copies ran while one was open for 7% -> 4% of each run, Pallas kernels for 0% -> 0%
where the time goes in v1:
time: 762 us; the launch traced here: 758 us
  matrix products  216 us (28%)
  local copies, waits for them, and re-layouts  205 us (27%)
  other arithmetic  117 us (15%)
  blocking collectives  105 us (14%)
  waiting for transfers between devices  99.5 us (13%)
  between operations  13.5 us (2%)
    dot_general x8, matrix products, pair_block(): jnp.dot(second_pick, table_slopes, precision=lax.Precision.HIGHEST, prefe...  108 us
    while x8, other arithmetic  101 us
    reshape x8, local copies, waits for them, and re-layouts, pair_block(): second_slopes = jnp.dot(second_pick, table_slopes, precision=lax.Precisio...  100 us
    all_to_all x1, blocking collectives, shards(): whole_slab = jnp.concatenate(lax.all_to_all(repeated, 'tm', 0, 0), axis=3)  75.1 us
    dot_general x8, matrix products, pair_block(): jnp.einsum('bcl,kcl->bk', convection, flat_modes, precision=lax.Precision...  70.9 us
    reduce_scatter x1, waiting for transfers between devices, shards(): lax.psum_scatter(pair_terms(owned, flat_modes, flat_slopes, factor, lax.a...  55.9 us
    ppermute x1, waiting for transfers between devices, padded(): lax.ppermute(lax.slice_in_dim(block, 0, width, axis=dim), axis, backward)  39.5 us
    dot_general x8, matrix products, pair_block(): jnp.dot(first_pick, table_modes, precision=lax.Precision.HIGHEST, preferr...  36.1 us
  transfers between devices with their start and end apart: 3, of which 3 were waited for; matrix products, arithmetic and copies ran while one was open for 4% of the time, Pallas kernels for 0%

profile of v1, /device:TPU:0, one launch (start us, length us, event | category | flops | bytes accessed | tf_op | source)
XLA Modules:
  0.0 758.3 jit_solution(5783641225199809103)
XLA Ops:
  8.9 30.3 %all_to_all.20 = f32[32,3,1,32,128]{4,0,2,1,3:T(8,128)S(1)} all-to-all(f32[32,3,1,32,128]{4,0,2,1,3:T(8,128)S(1)} %copy.74), channel_id=1, replica_groups=mesh['tm'=8,'space'=16] {'tm'}, dimensions={3} | all-to-all | bytes 3145728 | tf_op jit(solution)/shard_map/all_to_all | solution.py:69
  42.2 75.1 %all_to_all.21 = f32[8,128,3,1,4,128]{1,4,5,2,3,0:T(4,128)S(1)} all-to-all(f32[8,128,3,1,4,128]{1,4,5,2,3,0:T(4,128)S(1)} %stack.8), channel_id=1, replica_groups=mesh['tm'=8,'space'=16] {'tm'}, dimensions={0} | all-to-all | bytes 12582912 | tf_op jit(solution)/shard_map/all_to_all | solution.py:80
  118.3 6.7 copy.80
  127.3 6.5 copy.90
  133.8 6.6 copy.91
  141.2 5.9 fusion.15
  155.8 39.5 %collective-permute-done = f32[128,3,1,32,128]{0,3,4,1,2:T(8,128)} collective-permute-done((f32[128,3,1,32,128]{0,3,4,1,2:T(8,128)}, f32[128,3,1,32,128]{0,3,4,1,2:T(8,128)}, u32[]{:S(2)}, u32[]{:S(2)}) %collective-permute-start) | collective-permute-done | bytes 6291488 | tf_op jit(solution)/shard_map/ppermute | solution.py:17
  199.3 6.2 multiply_bitcast_fusion
  207.6 21.6 %copy.87 = f32[128,3,3,1,32,128]{0,5,4,2,1,3:T(8,128)} copy(f32[128,3,3,1,32,128]{0,4,5,2,3,1:T(8,128)S(1)} %pad_maximum_fusion) | data formatting | bytes 37748736 | tf_op jit(solution)/shard_map/stack | solution.py:26
  229.3 18.6 %copy.89 = f32[128,36864]{1,0:T(8,128)} copy(f32[128,36864]{0,1:T(8,128)} %bitcast.87) | data formatting | bytes 37748736 | tf_op jit(solution)/shard_map/while | solution.py:61
  247.9 446.9 %while.10 = (s32[]{:T(128)}, f32[8,64,128]{2,1,0:T(8,128)S(1)}, s32[8,64,2]{1,0,2:T(8,128)S(1)}, f32[128,36864]{1,0:T(8,128)}, f32[128,12288]{1,0:T(8,128)}, /*index=5*/f32[128,3,4096]{2,0,1:T(8,128)}, s32[]{:T(128)}) while((s32[]{:T(128)}, f32[8,64,128]{2,1,0:T(8,128)S(1)}, s32[8,64,2]{1,0,2:T(8,128)S(1)}, f32[128,36864]{1,0:T(8,128)}, ...), condition=%wide.region_1.2_spmd, body=%wide.region_0.1_spmd.sunk | while | flops 6043746304 | bytes 89164368 | solution.py:61
  247.9 13.5 %fusion.35 = f32[64,36864]{1,0:T(8,128)} fusion(f32[128,36864]{1,0:T(8,128)} %get-tuple-element.144, s32[64]{0:T(128)S(1)} %get-tuple-element.125), kind=kOutput, calls=%fused_computation.8.clone.1 | convolution fusion | flops 3623886848 | bytes 28311808 | tf_op jit(solution)/shard_map/while/body/eval_jaxpr/dot_general | solution.py:39
  261.4 12.6 %reshape.112 = f32[64,3,3,4096]{3,2,1,0:T(4,128)} reshape(f32[64,36864]{1,0:T(8,128)} %fusion.35) | data formatting | bytes 18874368 | tf_op jit(solution)/shard_map/while/body/eval_jaxpr/reshape | solution.py:44
  274.0 4.5 fusion.36
  282.3 12.6 %multiply_reduce_fusion.2 = f32[64,4096,3]{1,2,0:T(4,128)S(1)} fusion(f32[64,3,3,4096]{3,2,1,0:T(4,128)} %reshape.112, f32[64,4096,3]{1,2,0:T(4,128)} %bitcast.83), kind=kLoop, calls=%fused_computation.clone.1 | loop fusion | flops 3932160 | bytes 15728640 | tf_op jit(solution)/shard_map/while
  294.8 8.9 %fusion.37 = f32[8,64,128]{2,1,0:T(8,128)S(1)} fusion(f32[8,64,128]{2,1,0:T(8,128)S(1)} %get-tuple-element.135, s32[]{:T(128)} %get-tuple-element.134, f32[128,3,4096]{2,0,1:T(8,128)} %get-tuple-element.146, f32[64,4096,3]{1,2,0:T(4,128)S(1)} %multiply_reduce_fusion.2), kind=kOutput, calls=%fused_computation.5.clone.1 | convolution fusion | flops 1207959552 | bytes 10518532 | tf_op jit(solution)/shard_map/while/body/eval_jaxpr/bcl,kcl->bk/dot_general | solution.py:48
  303.8 13.5 %fusion.35 = f32[64,36864]{1,0:T(8,128)} fusion(f32[128,36864]{1,0:T(8,128)} %get-tuple-element.144, s32[64]{0:T(128)S(1)} %get-tuple-element.125), kind=kOutput, calls=%fused_computation.8.clone.1 | convolution fusion | flops 3623886848 | bytes 28311808 | tf_op jit(solution)/shard_map/while/body/eval_jaxpr/dot_general | solution.py:39
  317.3 12.6 %reshape.112 = f32[64,3,3,4096]{3,2,1,0:T(4,128)} reshape(f32[64,36864]{1,0:T(8,128)} %fusion.35) | data formatting | bytes 18874368 | tf_op jit(solution)/shard_map/while/body/eval_jaxpr/reshape | solution.py:44
  329.8 4.5 fusion.36
  338.1 12.6 %multiply_reduce_fusion.2 = f32[64,4096,3]{1,2,0:T(4,128)S(1)} fusion(f32[64,3,3,4096]{3,2,1,0:T(4,128)} %reshape.112, f32[64,4096,3]{1,2,0:T(4,128)} %bitcast.83), kind=kLoop, calls=%fused_computation.clone.1 | loop fusion | flops 3932160 | bytes 15728640 | tf_op jit(solution)/shard_map/while
  350.7 8.9 %fusion.37 = f32[8,64,128]{2,1,0:T(8,128)S(1)} fusion(f32[8,64,128]{2,1,0:T(8,128)S(1)} %get-tuple-element.135, s32[]{:T(128)} %get-tuple-element.134, f32[128,3,4096]{2,0,1:T(8,128)} %get-tuple-element.146, f32[64,4096,3]{1,2,0:T(4,128)S(1)} %multiply_reduce_fusion.2), kind=kOutput, calls=%fused_computation.5.clone.1 | convolution fusion | flops 1207959552 | bytes 10518532 | tf_op jit(solution)/shard_map/while/body/eval_jaxpr/bcl,kcl->bk/dot_general | solution.py:48
  359.6 13.5 %fusion.35 = f32[64,36864]{1,0:T(8,128)} fusion(f32[128,36864]{1,0:T(8,128)} %get-tuple-element.144, s32[64]{0:T(128)S(1)} %get-tuple-element.125), kind=kOutput, calls=%fused_computation.8.clone.1 | convolution fusion | flops 3623886848 | bytes 28311808 | tf_op jit(solution)/shard_map/while/body/eval_jaxpr/dot_general | solution.py:39
  373.1 12.6 %reshape.112 = f32[64,3,3,4096]{3,2,1,0:T(4,128)} reshape(f32[64,36864]{1,0:T(8,128)} %fusion.35) | data formatting | bytes 18874368 | tf_op jit(solution)/shard_map/while/body/eval_jaxpr/reshape | solution.py:44
  385.7 4.5 fusion.36
  394.0 12.6 %multiply_reduce_fusion.2 = f32[64,4096,3]{1,2,0:T(4,128)S(1)} fusion(f32[64,3,3,4096]{3,2,1,0:T(4,128)} %reshape.112, f32[64,4096,3]{1,2,0:T(4,128)} %bitcast.83), kind=kLoop, calls=%fused_computation.clone.1 | loop fusion | flops 3932160 | bytes 15728640 | tf_op jit(solution)/shard_map/while
  406.6 8.9 %fusion.37 = f32[8,64,128]{2,1,0:T(8,128)S(1)} fusion(f32[8,64,128]{2,1,0:T(8,128)S(1)} %get-tuple-element.135, s32[]{:T(128)} %get-tuple-element.134, f32[128,3,4096]{2,0,1:T(8,128)} %get-tuple-element.146, f32[64,4096,3]{1,2,0:T(4,128)S(1)} %multiply_reduce_fusion.2), kind=kOutput, calls=%fused_computation.5.clone.1 | convolution fusion | flops 1207959552 | bytes 10518532 | tf_op jit(solution)/shard_map/while/body/eval_jaxpr/bcl,kcl->bk/dot_general | solution.py:48
  415.5 13.5 %fusion.35 = f32[64,36864]{1,0:T(8,128)} fusion(f32[128,36864]{1,0:T(8,128)} %get-tuple-element.144, s32[64]{0:T(128)S(1)} %get-tuple-element.125), kind=kOutput, calls=%fused_computation.8.clone.1 | convolution fusion | flops 3623886848 | bytes 28311808 | tf_op jit(solution)/shard_map/while/body/eval_jaxpr/dot_general | solution.py:39
  429.0 12.6 %reshape.112 = f32[64,3,3,4096]{3,2,1,0:T(4,128)} reshape(f32[64,36864]{1,0:T(8,128)} %fusion.35) | data formatting | bytes 18874368 | tf_op jit(solution)/shard_map/while/body/eval_jaxpr/reshape | solution.py:44
  441.6 4.5 fusion.36
  449.9 12.6 %multiply_reduce_fusion.2 = f32[64,4096,3]{1,2,0:T(4,128)S(1)} fusion(f32[64,3,3,4096]{3,2,1,0:T(4,128)} %reshape.112, f32[64,4096,3]{1,2,0:T(4,128)} %bitcast.83), kind=kLoop, calls=%fused_computation.clone.1 | loop fusion | flops 3932160 | bytes 15728640 | tf_op jit(solution)/shard_map/while
  462.4 8.9 %fusion.37 = f32[8,64,128]{2,1,0:T(8,128)S(1)} fusion(f32[8,64,128]{2,1,0:T(8,128)S(1)} %get-tuple-element.135, s32[]{:T(128)} %get-tuple-element.134, f32[128,3,4096]{2,0,1:T(8,128)} %get-tuple-element.146, f32[64,4096,3]{1,2,0:T(4,128)S(1)} %multiply_reduce_fusion.2), kind=kOutput, calls=%fused_computation.5.clone.1 | convolution fusion | flops 1207959552 | bytes 10518532 | tf_op jit(solution)/shard_map/while/body/eval_jaxpr/bcl,kcl->bk/dot_general | solution.py:48
  471.3 13.5 %fusion.35 = f32[64,36864]{1,0:T(8,128)} fusion(f32[128,36864]{1,0:T(8,128)} %get-tuple-element.144, s32[64]{0:T(128)S(1)} %get-tuple-element.125), kind=kOutput, calls=%fused_computation.8.clone.1 | convolution fusion | flops 3623886848 | bytes 28311808 | tf_op jit(solution)/shard_map/while/body/eval_jaxpr/dot_general | solution.py:39
  484.9 12.6 %reshape.112 = f32[64,3,3,4096]{3,2,1,0:T(4,128)} reshape(f32[64,36864]{1,0:T(8,128)} %fusion.35) | data formatting | bytes 18874368 | tf_op jit(solution)/shard_map/while/body/eval_jaxpr/reshape | solution.py:44
  505.7 12.6 %multiply_reduce_fusion.2 = f32[64,4096,3]{1,2,0:T(4,128)S(1)} fusion(f32[64,3,3,4096]{3,2,1,0:T(4,128)} %reshape.112, f32[64,4096,3]{1,2,0:T(4,128)} %bitcast.83), kind=kLoop, calls=%fused_computation.clone.1 | loop fusion | flops 3932160 | bytes 15728640 | tf_op jit(solution)/shard_map/while
  518.3 8.9 %fusion.37 = f32[8,64,128]{2,1,0:T(8,128)S(1)} fusion(f32[8,64,128]{2,1,0:T(8,128)S(1)} %get-tuple-element.135, s32[]{:T(128)} %get-tuple-element.134, f32[128,3,4096]{2,0,1:T(8,128)} %get-tuple-element.146, f32[64,4096,3]{1,2,0:T(4,128)S(1)} %multiply_reduce_fusion.2), kind=kOutput, calls=%fused_computation.5.clone.1 | convolution fusion | flops 1207959552 | bytes 10518532 | tf_op jit(solution)/shard_map/while/body/eval_jaxpr/bcl,kcl->bk/dot_general | solution.py:48
  527.2 13.5 %fusion.35 = f32[64,36864]{1,0:T(8,128)} fusion(f32[128,36864]{1,0:T(8,128)} %get-tuple-element.144, s32[64]{0:T(128)S(1)} %get-tuple-element.125), kind=kOutput, calls=%fused_computation.8.clone.1 | convolution fusion | flops 3623886848 | bytes 28311808 | tf_op jit(solution)/shard_map/while/body/eval_jaxpr/dot_general | solution.py:39
  540.7 12.6 %reshape.112 = f32[64,3,3,4096]{3,2,1,0:T(4,128)} reshape(f32[64,36864]{1,0:T(8,128)} %fusion.35) | data formatting | bytes 18874368 | tf_op jit(solution)/shard_map/while/body/eval_jaxpr/reshape | solution.py:44
  561.6 12.6 %multiply_reduce_fusion.2 = f32[64,4096,3]{1,2,0:T(4,128)S(1)} fusion(f32[64,3,3,4096]{3,2,1,0:T(4,128)} %reshape.112, f32[64,4096,3]{1,2,0:T(4,128)} %bitcast.83), kind=kLoop, calls=%fused_computation.clone.1 | loop fusion | flops 3932160 | bytes 15728640 | tf_op jit(solution)/shard_map/while
  574.2 8.9 %fusion.37 = f32[8,64,128]{2,1,0:T(8,128)S(1)} fusion(f32[8,64,128]{2,1,0:T(8,128)S(1)} %get-tuple-element.135, s32[]{:T(128)} %get-tuple-element.134, f32[128,3,4096]{2,0,1:T(8,128)} %get-tuple-element.146, f32[64,4096,3]{1,2,0:T(4,128)S(1)} %multiply_reduce_fusion.2), kind=kOutput, calls=%fused_computation.5.clone.1 | convolution fusion | flops 1207959552 | bytes 10518532 | tf_op jit(solution)/shard_map/while/body/eval_jaxpr/bcl,kcl->bk/dot_general | solution.py:48
  583.1 13.5 %fusion.35 = f32[64,36864]{1,0:T(8,128)} fusion(f32[128,36864]{1,0:T(8,128)} %get-tuple-element.144, s32[64]{0:T(128)S(1)} %get-tuple-element.125), kind=kOutput, calls=%fused_computation.8.clone.1 | convolution fusion | flops 3623886848 | bytes 28311808 | tf_op jit(solution)/shard_map/while/body/eval_jaxpr/dot_general | solution.py:39
  596.6 12.6 %reshape.112 = f32[64,3,3,4096]{3,2,1,0:T(4,128)} reshape(f32[64,36864]{1,0:T(8,128)} %fusion.35) | data formatting | bytes 18874368 | tf_op jit(solution)/shard_map/while/body/eval_jaxpr/reshape | solution.py:44
  617.4 12.6 %multiply_reduce_fusion.2 = f32[64,4096,3]{1,2,0:T(4,128)S(1)} fusion(f32[64,3,3,4096]{3,2,1,0:T(4,128)} %reshape.112, f32[64,4096,3]{1,2,0:T(4,128)} %bitcast.83), kind=kLoop, calls=%fused_computation.clone.1 | loop fusion | flops 3932160 | bytes 15728640 | tf_op jit(solution)/shard_map/while
  630.0 8.9 %fusion.37 = f32[8,64,128]{2,1,0:T(8,128)S(1)} fusion(f32[8,64,128]{2,1,0:T(8,128)S(1)} %get-tuple-element.135, s32[]{:T(128)} %get-tuple-element.134, f32[128,3,4096]{2,0,1:T(8,128)} %get-tuple-element.146, f32[64,4096,3]{1,2,0:T(4,128)S(1)} %multiply_reduce_fusion.2), kind=kOutput, calls=%fused_computation.5.clone.1 | convolution fusion | flops 1207959552 | bytes 10518532 | tf_op jit(solution)/shard_map/while/body/eval_jaxpr/bcl,kcl->bk/dot_general | solution.py:48
  638.9 13.5 %fusion.35 = f32[64,36864]{1,0:T(8,128)} fusion(f32[128,36864]{1,0:T(8,128)} %get-tuple-element.144, s32[64]{0:T(128)S(1)} %get-tuple-element.125), kind=kOutput, calls=%fused_computation.8.clone.1 | convolution fusion | flops 3623886848 | bytes 28311808 | tf_op jit(solution)/shard_map/while/body/eval_jaxpr/dot_general | solution.py:39
  652.5 12.6 %reshape.112 = f32[64,3,3,4096]{3,2,1,0:T(4,128)} reshape(f32[64,36864]{1,0:T(8,128)} %fusion.35) | data formatting | bytes 18874368 | tf_op jit(solution)/shard_map/while/body/eval_jaxpr/reshape | solution.py:44
  673.3 12.6 %multiply_reduce_fusion.2 = f32[64,4096,3]{1,2,0:T(4,128)S(1)} fusion(f32[64,3,3,4096]{3,2,1,0:T(4,128)} %reshape.112, f32[64,4096,3]{1,2,0:T(4,128)} %bitcast.83), kind=kLoop, calls=%fused_computation.clone.1 | loop fusion | flops 3932160 | bytes 15728640 | tf_op jit(solution)/shard_map/while
  685.9 8.9 %fusion.37 = f32[8,64,128]{2,1,0:T(8,128)S(1)} fusion(f32[8,64,128]{2,1,0:T(8,128)S(1)} %get-tuple-element.135, s32[]{:T(128)} %get-tuple-element.134, f32[128,3,4096]{2,0,1:T(8,128)} %get-tuple-element.146, f32[64,4096,3]{1,2,0:T(4,128)S(1)} %multiply_reduce_fusion.2), kind=kOutput, calls=%fused_computation.5.clone.1 | convolution fusion | flops 1207959552 | bytes 10518532 | tf_op jit(solution)/shard_map/while/body/eval_jaxpr/bcl,kcl->bk/dot_general | solution.py:48
  695.5 55.9 %reduce-scatter.2.cloned.1.call-done = f32[32,128]{1,0:T(8,128)} async-done(((f32[512,128]{1,0:T(8,128)}), f32[32,128]{1,0:T(8,128)}) %reduce-scatter.2.cloned.1.call-update) | async-done | bytes 16400 | tf_op jit(solution)/shard_map/reduce_scatter | solution.py:88
  (55 shorter events, 73.1 us)
Async XLA Ops:
  6.5 33.0 %copy-start = (f32[256,128]{1,0:T(8,128)S(1)}, f32[256,128]{1,0:T(8,128)}, u32[]{:S(2)}) copy-start(f32[256,128]{1,0:T(8,128)} %param.6) | copy-start | bytes 393220
  6.5 744.9 %reduce-scatter.2.cloned.1.call-start = ((), (), s32[]{:S(2)}) async-start(), calls=%async_computation.3 | async-start | bytes 278528 | tf_op jit(solution)/shard_map/reduce_scatter | solution.py:88
  118.3 6.7 copy-start.2
  125.0 70.3 %collective-permute-start = (f32[128,3,1,32,128]{0,3,4,1,2:T(8,128)}, f32[128,3,1,32,128]{0,3,4,1,2:T(8,128)}, u32[]{:S(2)}, u32[]{:S(2)}) collective-permute-start(f32[128,3,1,32,128]{0,3,4,1,2:T(8,128)} %bitcast.14), channel_id=1, source_target_pairs={{1,0},{2,1},{3,2},{4,3},{5,4},{6,5},{7,6},{8,7},{9,8},{10,9},{11,1... | collective-permute-start | bytes 18874376 | tf_op jit(solution)/shard_map/ppermute | solution.py:17
  126.5 72.8 %collective-permute-start.1 = (f32[128,3,1,32,128]{0,3,4,1,2:T(8,128)}, f32[128,3,1,32,128]{0,3,4,1,2:T(8,128)}, u32[]{:S(2)}, u32[]{:S(2)}) collective-permute-start(f32[128,3,1,32,128]{0,3,4,1,2:T(8,128)} %bitcast.14), channel_id=1, source_target_pairs={{0,1},{1,2},{2,3},{3,4},{4,5},{5,6},{6,7},{7,8},{8,9},{9,10},{10,1... | collective-permute-start | bytes 18874376 | tf_op jit(solution)/shard_map/ppermute | solution.py:14
  694.8 56.7 %copy-start.1 = (f32[256,128]{1,0:T(8,128)S(1)}, f32[256,128]{1,0:T(8,128)}, u32[]{:S(2)}) copy-start(f32[256,128]{1,0:T(8,128)} %param.6) | copy-start | bytes 393220
Sparse Core Ops, SparseCore 0:
  695.7 55.7 reduce-scatter.1
